TPU v7x, 128 devices: a whole 4x4x4 slice. The times are simulated.
128 devices in a mesh: gz: 32 (over y, x, core), gy: 4 (over z).
Axes of the slice: x: 4, y: 4, z: 4, core: 2. Of those that a mesh axis runs over, the one named last changes fastest.
Arguments:
- init: float32 [128, 2048, 512], P('gz', None, 'gy'), may hold values from -6 to 6
- measured: float32 [4, 128, 2048, 512], P(None, None, 'gz', 'gy'), may hold values from -70 to 70
- mask: int32 [32, 8], replicated, may hold values from 0 to 1, as said below
- kernel_index: int32 [4, 8, 32], replicated, may hold values from 0 to 15
- kernels: float32 [16, 31], replicated, may hold values from 0.02 to 0.3
Outputs:
- solved: float32 [128, 2048, 512], P('gz', None, 'gy')
Inputs may be any that keep to these rules, and one draw needn't show every extreme that they name: `mask`: 1 marks a tissue block; in each aligned region of 64 x 128 lateral cells, whose blocks start at multiples of 64 and 128, exactly 1 block is 1.
All inputs are finite; a program needn't handle non-finite values.
Results may differ from a plain program's by a relative error of at most 0.0003.
Values sent between devices are 32-bit elements; how exact they have to be, the bound alone decides.
A program may use at most 128 MiB of HBM per device.

v0:
```python
import jax
import jax.numpy as jnp
from jax import lax
from jax.sharding import PartitionSpec as P

NZ = 128
XT = 64
YD = 128
BX = 64
BY = 64
ZBW = 16
TAPS = 31
VIEWS = 4
NK = 16
ITERS = 4
HALF = 15


HIGHEST = lax.Precision.HIGHEST
damping = 1.0


def blur_tables(kernel_index, kernels):
    onehot = (kernel_index[..., None] == jnp.arange(NK, dtype=jnp.int32)).astype(jnp.float32)
    tap_values = jnp.einsum("vabk,kt->vabt", onehot, kernels, precision=HIGHEST)
    row_taps = jnp.repeat(tap_values, ZBW, axis=1)
    depths = jnp.arange(NZ, dtype=jnp.int32)
    offset = depths[None, :] - depths[:, None] + HALF
    tap_select = (offset[:, :, None] == jnp.arange(TAPS, dtype=jnp.int32)).astype(jnp.float32)
    return jnp.einsum("vzbt,zwt->vbzw", row_taps, tap_select, precision=HIGHEST)


def conjugate(start_field, residual, operate):
    solved = start_field
    direction = residual
    norm_now = lax.psum(jnp.sum(residual * residual), ("gz", "gy"))
    for iteration in range(ITERS):
        image_field = operate(direction)
        curvature = lax.psum(jnp.sum(direction * image_field), ("gz", "gy"))
        step_size = norm_now / curvature
        solved = solved + step_size * direction
        residual = residual - step_size * image_field
        norm_next = lax.psum(jnp.sum(residual * residual), ("gz", "gy"))
        direction = residual + norm_next / norm_now * direction
        norm_now = norm_next
    return solved


def local(init, measured, mask, kernel_index, kernels):
    bands_here = XT // BX
    yblock_count = YD // BY
    tile_index = lax.axis_index("gz")
    row_index = lax.axis_index("gy")
    local_index = lax.dynamic_slice_in_dim(kernel_index, tile_index * bands_here, bands_here, 2)
    blur_mats = blur_tables(local_index, kernels)
    gram_mats = jnp.einsum("vbzw,vbzu->bwu", blur_mats, blur_mats, precision=HIGHEST)
    start_field = lax.all_to_all(init, "gz", split_axis=1, concat_axis=0, tiled=True)
    mask_block = lax.dynamic_slice(
        mask, (tile_index * bands_here, row_index * yblock_count), (bands_here, yblock_count)
    )
    tissue = jnp.repeat(jnp.repeat(mask_block.astype(jnp.float32), BX, axis=0), BY, axis=1)
    view_data = measured.reshape(VIEWS, NZ, bands_here, BX, YD)
    projected = jnp.einsum("vbzw,vzbxy->wbxy", blur_mats, view_data, precision=HIGHEST).reshape(
        NZ, XT, YD
    )

    def apply_gram(field):
        product = jnp.einsum(
            "bwz,zbxy->wbxy", gram_mats, field.reshape(NZ, bands_here, BX, YD), precision=HIGHEST
        )
        return product.reshape(NZ, XT, YD)

    def operate(field):
        return damping * field + tissue * apply_gram(field)

    residual = tissue * (projected - apply_gram(start_field))
    solved = conjugate(start_field, residual, operate)
    return lax.all_to_all(solved, "gz", split_axis=0, concat_axis=1, tiled=True)


def solution(mesh):
    return jax.shard_map(
        local,
        mesh=mesh,
        in_specs=(P("gz", None, "gy"), P(None, None, "gz", "gy"), P(), P(), P()),
        out_specs=P("gz", None, "gy"),
        check_vma=False,
    )
```

profile of v0, /device:TPU:1, one launch (start us, length us, event | category | flops | bytes accessed | tf_op | source)
XLA Modules:
  0.0 680.8 jit_solution(3410780401253675733)
XLA Ops:
  0.0 0.0 copy-start
  0.0 7.3 %copy.36 = f32[4,2048,128]{2,0,1:T(4,128)} copy(f32[4,2048,128]{2,1,0:T(8,128)} %param.5) | data formatting | bytes 8388608 | tf_op args[0]
  7.3 0.0 copy-start.5
  7.3 9.5 %all-to-all-start = ((f32[4,2048,128]{2,0,1:T(4,128)}), f32[4,2048,128]{2,0,1:T(4,128)}, u32[]{:S(2)}, u32[]{:S(2)}) async-start(f32[4,2048,128]{2,0,1:T(4,128)} %copy.36), calls=%async_computation | async-start | bytes 8388608 | tf_op jit(solution)/shard_map/all_to_all | solution.py:57
  16.8 0.9 convert_reduce_fusion
  17.6 0.1 broadcast_in_dim.8
  17.7 0.1 broadcast_in_dim.18
  17.8 0.0 copy-done
  17.8 0.2 dynamic-slice_reduce_fusion
  18.0 0.1 iota_compare_fusion.4
  18.1 0.0 copy-done.5
  18.1 0.1 fusion.39
  18.3 1.2 fusion.36
  19.5 0.1 copy.39
  19.7 0.4 fusion.47
  20.1 20.2 %fusion = f32[128,64,128,1]{2,0,3,1:T(8,128)} fusion(f32[4,128,64,128]{3,2,1,0:T(8,128)} %param.6, f32[4,128,128]{1,2,0:T(8,128)S(1)} %copy.39), kind=kOutput, calls=%fused_computation | convolution fusion | flops 6442450944 | bytes 21233664 | tf_op jit(solution)/shard_map/vbzw,vzbxy->wbxy/dot_general | solution.py:63
  40.2 26.9 %all-to-all-done = f32[4,2048,128]{2,0,1:T(4,128)} async-done(((f32[4,2048,128]{2,0,1:T(4,128)}), f32[4,2048,128]{2,0,1:T(4,128)}, u32[]{:S(2)}, u32[]{:S(2)}) %all-to-all-start) | async-done | bytes 4194336 | tf_op jit(solution)/shard_map/all_to_all | solution.py:57
  67.2 0.0 copy-start.4
  67.2 3.5 copy.37
  70.7 0.0 copy-start.3
  70.7 0.0 copy-done.4
  70.7 4.1 bitcast_subtract_fusion
  74.8 0.0 copy-done.3
  74.8 0.0 copy-start.2
  74.8 7.1 %multiply_reduce_fusion.5 = (f32[]{:T(128)}, f32[]{:T(128)}, f32[64,128,128]{1,2,0:T(8,128)}) fusion(f32[128,64,128]{2,0,1:T(8,128)S(1)} %bitcast_subtract_fusion, f32[128]{0:T(128)S(1)} %broadcast_in_dim.18, f32[128,128,1]{1,0,2:T(8,128)S(1)} %fusion.47), kind=kOutput, calls=%fused_computation.50 | convolution fusion | flops 1619001344 | bytes 8454664 | tf_op jit(solution)/shard_map/bwz,zbxy->wbxy/dot_general | solution.py:68
  81.9 0.0 copy-done.2
  81.9 67.0 %all-reduce = (f32[]{:T(128)}, f32[]{:T(128)}) all-reduce(f32[]{:T(128)} %get-tuple-element.6, f32[]{:T(128)} %get-tuple-element.5), channel_id=1, replica_groups=mesh['gz'=32,'gy'=4] {'gz','gy'}, use_global_device_ids=true, to_apply=%region_1.0 | all-reduce | flops 2 | bytes 16 | tf_op jit(solution)/shard_map/psum | solution.py:36
  150.2 5.2 multiply_reduce_fusion.4
  155.4 64.0 %psum.58 = f32[]{:T(128)} all-reduce(f32[]{:T(128)} %multiply_reduce_fusion.4), channel_id=1, replica_groups=mesh['gz'=32,'gy'=4] {'gz','gy'}, use_global_device_ids=true, to_apply=%region_5.0 | all-reduce | flops 1 | bytes 8 | tf_op jit(solution)/shard_map/psum | solution.py:43
  220.7 14.6 %multiply_reduce_fusion.3 = (f32[]{:T(128)}, f32[64,128,128]{1,2,0:T(8,128)}) fusion(f32[128]{0:T(128)S(1)} %broadcast_in_dim.18, f32[]{:T(128)S(6)} %div.22, f32[64,128,128]{1,2,0:T(8,128)} %get-tuple-element.9, f32[]{:T(128)S(6)} %div.21, f32[128,64,128]{2,0,1:T(8,128)} %copy-done.2, f32[128,128,1]{1,0,2:T(8,128)S(1)} %fusion.47), kind=kOutput, calls=%fused_computation.46 | convolution fusion | flops 1629487104 | bytes 12648972 | tf_op jit(solution)/shard_map/bwz,zbxy->wbxy/dot_general | solution.py:68
  235.3 62.5 %psum.59 = f32[]{:T(128)} all-reduce(f32[]{:T(128)} %get-tuple-element.10), channel_id=1, replica_groups=mesh['gz'=32,'gy'=4] {'gz','gy'}, use_global_device_ids=true, to_apply=%region_7.0 | all-reduce | flops 1 | bytes 8 | tf_op jit(solution)/shard_map/psum | solution.py:39
  299.2 7.1 %multiply_reduce_fusion.2 = f32[]{:T(128)} fusion(f32[64,128,128]{1,2,0:T(8,128)} %get-tuple-element.11, f32[]{:T(128)S(6)} %div.22, f32[]{:T(128)S(6)} %div.23, f32[64,128,128]{1,2,0:T(8,128)} %get-tuple-element.9, f32[]{:T(128)S(6)} %div.21, f32[128,64,128]{2,0,1:T(8,128)} %copy-done.2, f32[128]{0:T(128)S(1)} %broadcast_in_dim.18), kind=kLoop, calls=%fused_computation.44 | loop fusion | flops 13631487 | bytes 12583440 | tf_op jit(solution)/shard_map/reduce_sum | solution.py:43
  306.2 64.3 %psum.60 = f32[]{:T(128)} all-reduce(f32[]{:T(128)} %multiply_reduce_fusion.2), channel_id=1, replica_groups=mesh['gz'=32,'gy'=4] {'gz','gy'}, use_global_device_ids=true, to_apply=%region_9.0 | all-reduce | flops 1 | bytes 8 | tf_op jit(solution)/shard_map/psum | solution.py:43
  371.8 18.1 %multiply_reduce_fusion.1 = (f32[]{:T(128)}, f32[64,128,128]{1,2,0:T(8,128)}) fusion(f32[128]{0:T(128)S(1)} %broadcast_in_dim.18, f32[]{:T(128)S(6)} %div.24, f32[]{:T(128)S(6)} %div.22, f32[64,128,128]{1,2,0:T(8,128)} %get-tuple-element.9, f32[]{:T(128)S(6)} %div.21, f32[128,64,128]{2,0,1:T(8,128)} %copy-done.2, f32[64,128,128]{1,2,0:T(8,128)} %get-tuple-element.11, ...), kind=kOutput, calls=%fused_computation.41 | convolution fusion | flops 1642070016 | bytes 16843284 | tf_op jit(solution)/shard_map/bwz,zbxy->wbxy/dot_general | solution.py:68
  389.8 62.5 %psum.61 = f32[]{:T(128)} all-reduce(f32[]{:T(128)} %get-tuple-element.12), channel_id=1, replica_groups=mesh['gz'=32,'gy'=4] {'gz','gy'}, use_global_device_ids=true, to_apply=%region_11.0 | all-reduce | flops 1 | bytes 8 | tf_op jit(solution)/shard_map/psum | solution.py:39
  453.7 7.8 %multiply_reduce_fusion = f32[]{:T(128)} fusion(f32[64,128,128]{1,2,0:T(8,128)} %get-tuple-element.13, f32[128]{0:T(128)S(1)} %broadcast_in_dim.18, f32[]{:T(128)S(6)} %div.24, f32[]{:T(128)S(6)} %div.25, f32[]{:T(128)S(6)} %div.22, f32[64,128,128]{1,2,0:T(8,128)} %get-tuple-element.9, f32[]{:T(128)S(6)} %div.21, f32[128,64,128]{2,0,1:T(8,128)} %copy-done.2, ...), kind=kLoop, calls=%fused_computation.39 | loop fusion | flops 19922944 | bytes 16777752 | tf_op jit(solution)/shard_map/reduce_sum | solution.py:43
  461.4 64.3 %psum.62 = f32[]{:T(128)} all-reduce(f32[]{:T(128)} %multiply_reduce_fusion), channel_id=1, replica_groups=mesh['gz'=32,'gy'=4] {'gz','gy'}, use_global_device_ids=true, to_apply=%region_13.0 | all-reduce | flops 1 | bytes 8 | tf_op jit(solution)/shard_map/psum | solution.py:43
  527.0 20.0 %fusion.2 = f32[]{:T(128)} fusion(f32[]{:T(128)S(6)} %div.26, f32[128]{0:T(128)S(1)} %broadcast_in_dim.18, f32[128,128,1]{1,0,2:T(8,128)S(1)} %fusion.47, f32[64,128,128]{1,2,0:T(8,128)} %get-tuple-element.13, f32[]{:T(128)S(6)} %div.25, f32[]{:T(128)S(6)} %div.24, f32[64,128,128]{1,2,0:T(8,128)} %get-tuple-element.11, ...), kind=kOutput, calls=%fused_computation.3 | convolution fusion | flops 1654652928 | bytes 16843292 | tf_op jit(solution)/shard_map/bwz,zbxy->wbxy/dot_general | solution.py:68
  547.0 62.5 %psum.63 = f32[]{:T(128)} all-reduce(f32[]{:T(128)} %fusion.2), channel_id=1, replica_groups=mesh['gz'=32,'gy'=4] {'gz','gy'}, use_global_device_ids=true, to_apply=%region_15.0 | all-reduce | flops 1 | bytes 8 | tf_op jit(solution)/shard_map/psum | solution.py:39
  610.8 8.9 %multiply_add_fusion = f32[128,64,128]{2,0,1:T(8,128)S(1)} fusion(f32[128,64,128]{2,0,1:T(8,128)} %bitcast.267, f32[128,64,128]{2,0,1:T(8,128)} %copy-done.2, f32[]{:T(128)S(6)} %div.27, f32[]{:T(128)S(6)} %div.26, f32[]{:T(128)S(6)} %div.25, f32[]{:T(128)S(6)} %div.23, f32[]{:T(128)S(6)} %div.21, f32[128]{0:T(128)S(1)} %broadcast_in_dim.18, f32[]{:T(128)S(6)} %div.24, ...), kind=kLoop, calls=%fused_computation.36 | loop fusion | flops 28311552 | bytes 25166364 | tf_op jit(solution)/shard_map/add | solution.py:41
  619.7 2.4 copy.51
  622.2 55.9 %all_to_all.36 = f32[128,64,128]{2,1,0:T(8,128)S(1)} all-to-all(f32[128,64,128]{2,1,0:T(8,128)S(1)} %copy.51), channel_id=1, replica_groups=mesh['gz'=32,'gy'=4] {'gz'}, dimensions={0} | all-to-all | bytes 8388608 | tf_op jit(solution)/shard_map/all_to_all | solution.py:78
  678.1 0.0 copy-start.1
  678.1 2.3 copy.52
  680.4 0.0 copy-done.1
  (2 shorter events, 0.1 us)
Async XLA Ops:
  0.0 17.8 %copy-start = (s32[4,8,32]{2,1,0:T(8,128)S(1)}, s32[4,8,32]{2,1,0:T(8,128)}, u32[]{:S(2)}) copy-start(s32[4,8,32]{2,1,0:T(8,128)} %param.8) | copy-start | bytes 12292
  7.3 10.8 %copy-start.5 = (f32[16,31]{1,0:T(8,128)S(1)}, f32[16,31]{1,0:T(8,128)}, u32[]{:S(2)}) copy-start(f32[16,31]{1,0:T(8,128)} %param.9) | copy-start | bytes 5956
  7.3 59.9 %all-to-all-start = ((f32[4,2048,128]{2,0,1:T(4,128)}), f32[4,2048,128]{2,0,1:T(4,128)}, u32[]{:S(2)}, u32[]{:S(2)}) async-start(f32[4,2048,128]{2,0,1:T(4,128)} %copy.36), calls=%async_computation | async-start | bytes 8388608 | tf_op jit(solution)/shard_map/all_to_all | solution.py:57
  67.2 3.5 copy-start.4
  70.7 4.1 copy-start.3
  74.8 7.1 %copy-start.2 = (f32[128,64,128]{2,0,1:T(8,128)}, f32[128,64,128]{2,0,1:T(8,128)S(1)}, u32[]{:S(2)}) copy-start(f32[128,64,128]{2,0,1:T(8,128)S(1)} %bitcast_subtract_fusion) | copy-start | bytes 12582916
  678.1 2.3 copy-start.1
where the time goes:
time: 685 us; the launch traced here: 681 us
  blocking collectives  503 us (73%)
  matrix products  85.8 us (13%)
  other arithmetic  29.9 us (4%)
  waiting for transfers between devices  26.9 us (4%)
  local copies, waits for them, and re-layouts  16.1 us (2%)
  between operations  9.51 us (1%)
  starting transfers between devices  9.48 us (1%)
    psum x3, blocking collectives, conjugate(): norm_next = lax.psum(jnp.sum(residual * residual), ('gz', 'gy'))  193 us
    psum x3, blocking collectives, conjugate(): curvature = lax.psum(jnp.sum(direction * image_field), ('gz', 'gy'))  188 us
    psum x1, blocking collectives, conjugate(): norm_now = lax.psum(jnp.sum(residual * residual), ('gz', 'gy'))  67 us
    dot_general x5, matrix products, apply_gram(): jnp.einsum('bwz,zbxy->wbxy', gram_mats, field.reshape(NZ, bands_here, BX,...  63.9 us
    all_to_all x1, blocking collectives, local(): return lax.all_to_all(solved, 'gz', split_axis=0, concat_axis=1, tiled=True)  55.9 us
    all_to_all x1, waiting for transfers between devices, local(): lax.all_to_all(init, 'gz', split_axis=1, concat_axis=0, tiled=True)  26.9 us
    dot_general x1, matrix products, local(): jnp.einsum('vbzw,vzbxy->wbxy', blur_mats, view_data, precision=HIGHEST)  20.2 us
    reduce_sum x3, other arithmetic, conjugate(): norm_next = lax.psum(jnp.sum(residual * residual), ('gz', 'gy'))  20 us
  transfers between devices with their start and end apart: 1, of which 1 were waited for; matrix products, arithmetic and copies ran while one was open for 3% of the time, Pallas kernels for 0%

commit v1 on v0

v1 whole, which is shorter than its diff:
```python
import jax
import jax.numpy as jnp
from jax import lax
from jax.experimental import pallas as pl
from jax.experimental.pallas import tpu as pltpu
from jax.sharding import PartitionSpec as P

NZ = 128
XT = 64
YD = 128
ZBW = 16
TAPS = 31
VIEWS = 4
NK = 16
ITERS = 4
HALF = 15
ZBANDS = 8
TILES = 32
RINGX, RINGY, CORES = 4, 4, 2
DEPTHS = 4
CHUNKS = 4
ROWS = 8
PIECE = DEPTHS * ROWS
PART = TILES * PIECE

MESH = pl.DeviceIdType.MESH
HIGHEST = lax.Precision.HIGHEST
F32 = jnp.float32
BF16 = jnp.bfloat16


def away(d, n):
    return min(d, n - d)


OFFSETS = sorted(
    ((dx, dy, dc) for dx in range(RINGX) for dy in range(RINGY) for dc in range(CORES)),
    key=lambda t: (-(away(t[0], RINGX) + away(t[1], RINGY)), t),
)
OFFSETS.remove((0, 0, 0))
FAR = len(OFFSETS)


def dot(a, b, precision=None):
    return jnp.dot(a, b, precision=precision, preferred_element_type=F32)


def dot_nt(a, b):
    return lax.dot_general(
        a, b, (((1,), (1,)), ((), ())), precision=HIGHEST, preferred_element_type=F32
    )


def halves(value):
    high = value.astype(BF16)
    return high, (value - high.astype(F32)).astype(BF16)


def pack(low_rows, high_rows, upper, lane):
    rolled = pltpu.roll(jnp.where(upper, low_rows, high_rows), 64, 1)
    return jnp.where(
        lane < 64, jnp.where(upper, rolled, low_rows), jnp.where(upper, high_rows, rolled)
    )


def mix(row, low_rows, high_rows, upper, lane):
    rolled = pltpu.roll(row, 64, 1)
    left = lane < 64
    spread_low = jnp.where(upper, rolled, row)
    spread_high = jnp.where(upper, row, rolled)
    tissue = jnp.logical_xor(left, upper)
    return jnp.where(tissue, spread_low, low_rows), jnp.where(tissue, spread_high, high_rows)


def cg_weights(moments, centre, half):
    product = [
        [0.5 * (moments[i + j] + moments[abs(i - j)]) for j in range(ITERS + 1)]
        for i in range(ITERS)
    ]

    def apply(a):
        out = [centre * value for value in a] + [None]

        def put(j, value):
            out[j] = value if out[j] is None else out[j] + value

        for j, value in enumerate(a):
            if j == 0:
                put(1, half * value)
            else:
                put(j + 1, 0.5 * half * value)
                put(j - 1, 0.5 * half * value)
        return out

    def square(a):
        total = None
        for i in range(len(a)):
            row = a[i] * product[i][i]
            for j in range(i + 1, len(a)):
                row = row + 2.0 * a[j] * product[i][j]
            total = a[i] * row if total is None else total + a[i] * row
        return total

    def inner(a, b):
        total = None
        for i in range(len(a)):
            row = None
            for j in range(len(b)):
                term = b[j] * product[i][j]
                row = term if row is None else row + term
            total = a[i] * row if total is None else total + a[i] * row
        return total

    one = jnp.ones_like(moments[0])
    residual, direction, step = [one], [one], []
    norm_now = moments[0]
    for iteration in range(ITERS):
        image = apply(direction)
        alpha = norm_now / inner(direction, image)
        step = [
            alpha * d if j >= len(step) else step[j] + alpha * d for j, d in enumerate(direction)
        ]
        if iteration == ITERS - 1:
            return step
        residual = [
            -alpha * v if j >= len(residual) else residual[j] - alpha * v
            for j, v in enumerate(image)
        ]
        norm_next = square(residual)
        ratio = norm_next / norm_now
        direction = [
            r if j >= len(direction) else r + ratio * direction[j] for j, r in enumerate(residual)
        ]
        norm_now = norm_next


def solve_kernel(
    init_ref, measured_ref, mask_ref, index_ref, index_row_ref, kernels_ref, prior,
    views, sent, field, back, solved, resid, taps, kpad, blur_rows, blur_ops, gram_ops, step_ops,
    cheb, total, part, part_z, part_g, sum_z,
    prior_sem, view_sem, send_sem, recv_sem, back_sem, ret_sem, z_send, z_recv, g_send, g_recv,
):
    me = lax.axis_index("gz")
    row = lax.axis_index("gy")
    my_core = lax.rem(me, CORES)
    my_x = lax.rem(lax.div(me, CORES), RINGX)
    my_y = lax.div(me, CORES * RINGX)

    def peer(offset):
        dx, dy, dc = offset
        return (
            lax.rem(my_y + dy, RINGY) * RINGX + lax.rem(my_x + dx, RINGX)
        ) * CORES + lax.rem(my_core + dc, CORES)

    def prior_copy(d):
        return pltpu.make_async_copy(init_ref.at[d], prior.at[d], prior_sem.at[d])

    def view_copy(i):
        return pltpu.make_async_copy(
            measured_ref.at[:, pl.ds(i * ROWS, ROWS), :], views.at[i], view_sem.at[i]
        )

    for d in range(DEPTHS):
        prior_copy(d).start()

    barrier = pltpu.get_barrier_semaphore()
    for offset in OFFSETS:
        pl.semaphore_signal(barrier, inc=1, device_id=(peer(offset), row), device_id_type=MESH)
    for dz in range(1, 4):
        pl.semaphore_signal(
            barrier, inc=1, device_id=(me, lax.rem(row + dz, 4)), device_id_type=MESH
        )

    lane8 = lax.broadcasted_iota(jnp.int32, (ROWS, 128), 1)
    for d in range(DEPTHS):
        prior_copy(d).wait()
    for c in range(CHUNKS):
        for i in (c, c + CHUNKS):
            view_copy(i).start()

    def pack_chunk(c):
        @pl.loop(0, TILES)
        def _(p):
            upper = jnp.full((ROWS, 128), mask_ref[2 * row + 1, p], jnp.int32) != 0
            for d in range(DEPTHS):
                low = pl.multiple_of(p * XT + c * ROWS, ROWS)
                high = pl.multiple_of(p * XT + c * ROWS + XT // 2, ROWS)
                packed = pack(
                    prior[d, pl.ds(low, ROWS), :], prior[d, pl.ds(high, ROWS), :], upper, lane8
                )
                sent[c, pl.ds(pl.multiple_of(p * PIECE + d * ROWS, ROWS), ROWS), :] = packed

    def send_chunk(source, target, c, send, recv):
        for offset in OFFSETS:
            p = peer(offset)
            pltpu.make_async_remote_copy(
                src_ref=source.at[c, pl.ds(pl.multiple_of(p * PIECE, PIECE), PIECE)],
                dst_ref=target.at[c, pl.ds(pl.multiple_of(me * PIECE, PIECE), PIECE)],
                send_sem=send.at[c],
                recv_sem=recv.at[c],
                device_id=(p, row),
                device_id_type=MESH,
            ).start()

    def chunk_copy(source, target, c, send, recv):
        return pltpu.make_async_remote_copy(
            src_ref=source.at[c, pl.ds(0, FAR * PIECE)],
            dst_ref=target.at[c, pl.ds(0, FAR * PIECE)],
            send_sem=send.at[c],
            recv_sem=recv.at[c],
            device_id=(peer(OFFSETS[0]), row),
            device_id_type=MESH,
        )

    pack_chunk(0)
    pl.semaphore_wait(barrier, FAR + 3)

    @pl.loop(0, CHUNKS)
    def _(c):
        send_chunk(sent, field, c, send_sem, recv_sem)

        @pl.when(c < CHUNKS - 1)
        def _():
            pack_chunk(c + 1)

    own = pl.ds(pl.multiple_of(me * PIECE, PIECE), PIECE)
    for c in range(CHUNKS):
        field[c, own, :] = sent[c, own, :]

    lane = lax.broadcasted_iota(jnp.int32, (NZ, NZ), 1)
    depth = lax.broadcasted_iota(jnp.int32, (NZ, NZ), 0)
    kpad[...] = jnp.zeros((NK, 128), F32)
    kpad[:, 0:TAPS] = kernels_ref[...]
    for v in range(VIEWS):
        for band in range(ZBANDS):
            k = index_ref[v * ZBANDS + band, me]
            taps[pl.ds((v * ZBANDS + band) * ZBW, ZBW), :] = jnp.broadcast_to(
                kpad[pl.ds(k, 1), :], (ZBW, 128)
            )
    near = jnp.abs(lane - depth) <= HALF
    for v in range(VIEWS):
        at = pl.ds(v * NZ, NZ)
        mat = jnp.where(
            near, pltpu.roll(taps[at, :], 128 - HALF, 1, stride=1, stride_axis=0), 0.0
        )
        turned = mat.T
        blur_rows[at, :] = mat
        high, low = halves(turned)
        blur_ops[0:NZ, at] = high
        blur_ops[NZ:, at] = low
        taps[at, :] = turned
    grams = dot(taps[0:NZ, :], blur_rows[0:NZ, :], HIGHEST)
    for v in range(1, VIEWS):
        at = pl.ds(v * NZ, NZ)
        grams = grams + dot(taps[at, :], blur_rows[at, :], HIGHEST)
    high, low = halves(grams)
    gram_ops[0:NZ, 0:NZ] = high
    gram_ops[0:NZ, NZ:] = high
    gram_ops[NZ:, 0:NZ] = low
    gram_ops[NZ:, NZ:] = jnp.zeros((NZ, NZ), BF16)

    bins = lax.broadcasted_iota(jnp.int32, (NK, TILES), 0)
    span = lax.broadcasted_iota(jnp.int32, (3 * ZBW, 128), 0)
    tap = lax.broadcasted_iota(jnp.int32, (3 * ZBW, 128), 1)
    window = jnp.where(jnp.logical_and(tap >= span - ZBW, tap < span), 1.0, 0.0)
    sums = dot_nt(window, kpad[...]) * dot_nt(jnp.ones((3 * ZBW, 128), F32), kpad[...])
    spreads = []
    for band in range(ZBANDS):
        counts = jnp.zeros((NK, TILES), F32)
        for v in range(VIEWS):
            at = v * ZBANDS + band
            counts = counts + jnp.where(index_row_ref[at : at + 1, :] == bins, 1.0, 0.0)
        spreads.append(dot(sums, counts, HIGHEST))
    row_sums = None
    for band in range(ZBANDS):
        here = spreads[band][ZBW : 2 * ZBW, :]
        if band > 0:
            here = here + spreads[band - 1][2 * ZBW :, :]
        if band < ZBANDS - 1:
            here = here + spreads[band + 1][0:ZBW, :]
        row_sums = here if row_sums is None else jnp.maximum(row_sums, here)
    bound = jnp.max(jnp.max(row_sums, axis=0, keepdims=True), axis=1, keepdims=True)
    half = jnp.broadcast_to(0.5001 * bound, (1, 128))
    centre = 1.0 + half

    eye = jnp.where(lane == depth, 1.0, 0.0)
    cheb[0] = eye
    cheb[1] = grams / half - eye
    cheb[2] = 2.0 * dot(cheb[1], cheb[1], HIGHEST) - eye
    cheb[3] = 2.0 * dot(cheb[1], cheb[2], HIGHEST) - cheb[1]
    cheb[4] = 2.0 * dot(cheb[2], cheb[2], HIGHEST) - eye
    cheb[5] = 2.0 * dot(cheb[2], cheb[3], HIGHEST) - cheb[1]
    cheb[6] = 2.0 * dot(cheb[3], cheb[3], HIGHEST) - eye
    cheb[7] = 2.0 * dot(cheb[3], cheb[4], HIGHEST) - cheb[1]

    mine = jnp.full((NZ, 128), mask_ref[2 * row + 1, me], jnp.int32) != 0

    for i in range(2 * CHUNKS):
        view_copy(i).wait()

    @pl.loop(0, CHUNKS)
    def _(c):
        @pl.loop(0, ROWS // 2)
        def _(pair):
            product = None
            for v in range(VIEWS):
                sides = []
                for r in range(2):
                    at = pl.ds(pair * 2 + r, NZ, stride=ROWS)
                    lows = views.at[c, pl.ds(v * NZ, NZ)].reshape(NZ * ROWS, 128)[at, :]
                    highs = views.at[c + CHUNKS, pl.ds(v * NZ, NZ)].reshape(NZ * ROWS, 128)[at, :]
                    sides.append(pack(lows, highs, mine, lane))
                high, low = halves(jnp.concatenate(sides, axis=1))
                ops = blur_ops[:, pl.ds(v * NZ, NZ)]
                both = dot(ops, high)
                term = both[0:NZ] + both[NZ:] + dot(ops[0:NZ], low)
                product = term if product is None else product + term
            resid[c * (ROWS // 2) + pair] = product

    def columns(c, pair):
        sides = [field[c, pl.ds(pair * 2 + r, NZ, stride=ROWS), :] for r in range(2)]
        return jnp.concatenate(sides, axis=1)

    def times(ops, value):
        high, low = halves(value)
        both = dot(ops[...], jnp.concatenate([high, low], axis=0))
        return both[0:NZ] + both[NZ:]

    total[...] = jnp.zeros((NZ, NZ), F32)

    @pl.loop(0, CHUNKS)
    def _(c):
        chunk_copy(sent, field, c, send_sem, recv_sem).wait_recv()

        @pl.loop(0, ROWS // 2)
        def _(pair):
            at = c * (ROWS // 2) + pair
            first = resid[at] - times(gram_ops, columns(c, pair))
            resid[at] = first
            total[...] += dot_nt(first, first)

    lane1 = lax.broadcasted_iota(jnp.int32, (1, 128), 1)
    local = jnp.zeros((1, 128), F32)
    for k in range(2 * ITERS):
        value = jnp.sum(cheb[k] * total[...], axis=0, keepdims=True)
        local = jnp.where(lane1 == k, jnp.sum(value, axis=1, keepdims=True), local)
    part[0] = local
    part_z[row] = local
    hops = []
    for dz in range(1, 4):
        copy = pltpu.make_async_remote_copy(
            src_ref=part.at[0],
            dst_ref=part_z.at[row],
            send_sem=z_send.at[dz - 1],
            recv_sem=z_recv.at[dz - 1],
            device_id=(me, lax.rem(row + dz, 4)),
            device_id_type=MESH,
        )
        copy.start()
        hops.append(copy)
    for copy in hops:
        copy.wait()
    along = (part_z[0] + part_z[1]) + (part_z[2] + part_z[3])
    sum_z[0] = along
    part_g[me] = along
    for offset in OFFSETS:
        p = peer(offset)
        pltpu.make_async_remote_copy(
            src_ref=sum_z.at[0],
            dst_ref=part_g.at[me],
            send_sem=g_send.at[0],
            recv_sem=g_recv.at[0],
            device_id=(p, row),
            device_id_type=MESH,
        ).start()
    everyone = pltpu.make_async_remote_copy(
        src_ref=part_g.at[pl.ds(0, FAR)],
        dst_ref=part_g.at[pl.ds(0, FAR)],
        send_sem=g_send.at[0],
        recv_sem=g_recv.at[0],
        device_id=(peer(OFFSETS[0]), row),
        device_id_type=MESH,
    )
    everyone.wait_recv()
    whole = jnp.sum(part_g[...], axis=0)
    moments = [
        jnp.broadcast_to(
            jnp.sum(jnp.where(lane1 == k, whole, 0.0), axis=1, keepdims=True), (1, 128)
        )
        for k in range(2 * ITERS)
    ]
    weights = cg_weights(moments, centre, half)

    poly = weights[0] * cheb[0]
    for j in range(1, ITERS):
        poly = poly + weights[j] * cheb[j]
    high, low = halves(poly)
    step_ops[0:NZ, 0:NZ] = high
    step_ops[0:NZ, NZ:] = high
    step_ops[NZ:, 0:NZ] = low
    step_ops[NZ:, NZ:] = jnp.zeros((NZ, NZ), BF16)

    @pl.loop(0, CHUNKS)
    def _(c):
        @pl.loop(0, ROWS // 2)
        def _(pair):
            moved = columns(c, pair) + times(step_ops, resid[c * (ROWS // 2) + pair])
            for r in range(2):
                back[c, pl.ds(pair * 2 + r, NZ, stride=ROWS), :] = moved[:, r * 128 : (r + 1) * 128]

        solved[c, own, :] = back[c, own, :]
        send_chunk(back, solved, c, back_sem, ret_sem)

    @pl.loop(0, CHUNKS)
    def _(c):
        chunk_copy(back, solved, c, back_sem, ret_sem).wait_recv()

        @pl.loop(0, TILES)
        def _(b):
            upper = jnp.full((ROWS, 128), mask_ref[2 * row + 1, b], jnp.int32) != 0
            for d in range(DEPTHS):
                low = pl.ds(pl.multiple_of(b * XT + c * ROWS, ROWS), ROWS)
                high = pl.ds(pl.multiple_of(b * XT + c * ROWS + XT // 2, ROWS), ROWS)
                prior[d, low, :], prior[d, high, :] = mix(
                    solved[c, pl.ds(pl.multiple_of(b * PIECE + d * ROWS, ROWS), ROWS), :],
                    prior[d, low, :], prior[d, high, :], upper, lane8,
                )

    everyone.wait_send()
    for c in range(CHUNKS):
        chunk_copy(sent, field, c, send_sem, recv_sem).wait_send()
        chunk_copy(back, solved, c, back_sem, ret_sem).wait_send()


def place_kernel(solved_ref, out_ref, sem):
    copies = [pltpu.make_async_copy(solved_ref.at[d], out_ref.at[d], sem.at[d]) for d in range(DEPTHS)]
    for copy in copies:
        copy.start()
    for copy in copies:
        copy.wait()


def local(init, measured, mask, kernel_index, kernels):
    nx = TILES * XT
    smem = pl.BlockSpec(memory_space=pltpu.SMEM)
    vmem = pl.BlockSpec(memory_space=pltpu.VMEM)
    hbm = pl.BlockSpec(memory_space=pltpu.HBM)
    dma = pltpu.SemaphoreType.DMA
    solved = pl.pallas_call(
        solve_kernel,
        out_shape=jax.ShapeDtypeStruct((DEPTHS, nx, 128), F32),
        in_specs=[hbm, hbm, smem, smem, vmem, vmem],
        out_specs=vmem,
        scratch_shapes=[
            pltpu.VMEM((2 * CHUNKS, VIEWS * NZ, ROWS, 128), F32),
            pltpu.VMEM((CHUNKS, PART, 128), F32),
            pltpu.VMEM((CHUNKS, PART, 128), F32),
            pltpu.VMEM((CHUNKS, PART, 128), F32),
            pltpu.VMEM((CHUNKS, PART, 128), F32),
            pltpu.VMEM((CHUNKS * ROWS // 2, NZ, 256), F32),
            pltpu.VMEM((VIEWS * NZ, 128), F32),
            pltpu.VMEM((NK, 128), F32),
            pltpu.VMEM((VIEWS * NZ, NZ), F32),
            pltpu.VMEM((2 * NZ, VIEWS * NZ), BF16),
            pltpu.VMEM((2 * NZ, 2 * NZ), BF16),
            pltpu.VMEM((2 * NZ, 2 * NZ), BF16),
            pltpu.VMEM((2 * ITERS, NZ, NZ), F32),
            pltpu.VMEM((NZ, NZ), F32),
            pltpu.VMEM((1, 1, 128), F32),
            pltpu.VMEM((4, 1, 128), F32),
            pltpu.VMEM((TILES, 1, 128), F32),
            pltpu.VMEM((1, 1, 128), F32),
            dma((DEPTHS,)),
            dma((2 * CHUNKS,)),
            dma((CHUNKS,)),
            dma((CHUNKS,)),
            dma((CHUNKS,)),
            dma((CHUNKS,)),
            dma((3,)),
            dma((3,)),
            dma((1,)),
            dma((1,)),
        ],
        compiler_params=pltpu.CompilerParams(
            collective_id=0, has_side_effects=True, vmem_limit_bytes=48 << 20
        ),
        name="solve",
    )(
        init,
        measured.reshape(VIEWS * NZ, XT, YD),
        mask.T,
        kernel_index.reshape(VIEWS * ZBANDS, TILES),
        kernel_index.reshape(VIEWS * ZBANDS, TILES),
        kernels,
    )
    return pl.pallas_call(
        place_kernel,
        out_shape=jax.ShapeDtypeStruct((DEPTHS, nx, 128), F32),
        in_specs=[vmem],
        out_specs=hbm,
        scratch_shapes=[dma((DEPTHS,))],
        compiler_params=pltpu.CompilerParams(vmem_limit_bytes=8 << 20),
        name="place",
    )(solved)


def solution(mesh):
    return jax.shard_map(
        local,
        mesh=mesh,
        in_specs=(P("gz", None, "gy"), P(None, None, "gz", "gy"), P(), P(), P()),
        out_specs=P("gz", None, "gy"),
        check_vma=False,
    )
```

time: 685 us -> 79.2 us (0.12)
  blocking collectives: 503 us -> 0 us
  matrix products: 85.8 us -> 0 us
  Pallas kernels: 0 us -> 76.5 us
  other arithmetic: 29.9 us -> 0 us
  waiting for transfers between devices: 26.9 us -> 0 us
  local copies, waits for them, and re-layouts: 16.1 us -> 2.1 us
  between operations: 9.51 us -> 0.01 us
  starting transfers between devices: 9.48 us -> 0 us
    psum x7 -> x0, blocking collectives: 447 us -> none  [the longest x3 193 us: conjugate(): norm_next = lax.psum(jnp.sum(residual * residual), ('gz', 'gy'))]
    dot_general x9 -> x0, matrix products: 85.8 us -> none  [the longest x5 63.9 us: apply_gram(): jnp.einsum('bwz,zbxy->wbxy', gram_mats, field.reshape(NZ, bands_here, BX,...]
    pallas_call x0 -> x2, Pallas kernels: none -> 76.5 us  [the longest x1 74.5 us: local(): pl.pallas_call(solve_kernel, out_shape=jax.ShapeDtypeStruct((DEPTHS, nx,...]
    all_to_all x1 -> x0, blocking collectives: 55.9 us -> none  [local(): return lax.all_to_all(solved, 'gz', split_axis=0, concat_axis=1, tiled=True)]
    all_to_all x1 -> x0, waiting for transfers between devices: 26.9 us -> none  [local(): lax.all_to_all(init, 'gz', split_axis=1, concat_axis=0, tiled=True)]
    reduce_sum x3 -> x0, other arithmetic: 20 us -> none  [conjugate(): norm_next = lax.psum(jnp.sum(residual * residual), ('gz', 'gy'))]
    all_to_all x1 -> x0, starting transfers between devices: 9.48 us -> none  [local(): lax.all_to_all(init, 'gz', split_axis=1, concat_axis=0, tiled=True)]
    add x2 -> x0, other arithmetic: 8.92 us -> none  [the longest x1 8.91 us: conjugate(): solved = solved + step_size * direction]
  transfers between devices with their start and end apart: 1 -> 0, of which waited for: 1 -> 0; matrix products, arithmetic and copies ran while one was open for 3% -> 0% of each run, Pallas kernels for 0% -> 0%
where the time goes in v1:
time: 79.2 us; the launch traced here: 78.7 us
  Pallas kernels  76.5 us (97%)
  local copies, waits for them, and re-layouts  2.1 us (3%)
    pallas_call x1, Pallas kernels, local(): pl.pallas_call(solve_kernel, out_shape=jax.ShapeDtypeStruct((DEPTHS, nx,...  74.5 us
    unnamed x6, local copies, waits for them, and re-layouts  2.1 us
    pallas_call x1, Pallas kernels, local(): pl.pallas_call(place_kernel, out_shape=jax.ShapeDtypeStruct((DEPTHS, nx,...  2.04 us

profile of v1, /device:TPU:1, one launch (start us, length us, event | category | flops | bytes accessed | tf_op | source)
XLA Modules:
  0.0 78.7 jit_solution(14351002501382008341)
XLA Ops:
  0.0 0.0 copy-start
  0.0 0.7 copy-done
  0.7 0.0 copy-start.1
  0.7 0.7 copy-done.1
  1.4 0.0 copy-start.2
  1.4 0.7 copy-done.2
  2.1 74.5 %solve.1.solved_ref = f32[4,2048,128]{2,1,0:T(8,128)S(1)} custom-call(f32[4,2048,128]{2,1,0:T(8,128)} %init_ref.1, f32[512,64,128]{2,1,0:T(8,128)} %bitcast.6, s32[8,32]{1,0:T(8,128)S(1)} %bitcast.5, s32[32,32]{1,0:T(8,128)S(1)} %bitcast.3, s32[32,32]{1,0:T(8,128)S(1)} %bitcast.4, f32[16,31]{1,0:T(8,128)S(1)} %copy-done.1), custom_call_target="tpu_custom_call" | custom-call | tf_op jit(solution)/shard_map/solve/pallas_call | solution.py:449
  76.6 2.0 %place.1 = f32[4,2048,128]{2,1,0:T(8,128)} custom-call(f32[4,2048,128]{2,1,0:T(8,128)S(1)} %solve.1.solved_ref), custom_call_target="tpu_custom_call" | custom-call | tf_op jit(solution)/shard_map/place/pallas_call | solution.py:496
Async XLA Ops:
  0.0 0.7 copy-start
  0.7 0.7 copy-start.1
  1.4 0.7 copy-start.2

commit v2 on v1

--- a/solution.py
+++ b/solution.py
@@ -15,6 +15,7 @@
 ITERS = 4
 HALF = 15
 ZBANDS = 8
+NY_BLOCKS = 8
 TILES = 32
 RINGX, RINGY, CORES = 4, 4, 2
 DEPTHS = 4
@@ -135,10 +136,10 @@
 
 
 def solve_kernel(
-    init_ref, measured_ref, mask_ref, index_ref, index_row_ref, kernels_ref, prior,
-    views, sent, field, back, solved, resid, taps, kpad, blur_rows, blur_ops, gram_ops, step_ops,
+    init_ref, measured_ref, mask_hbm, index_hbm, kernels_hbm, prior,
+    mask_ref, index_ref, index_row_ref, kernels_ref, views, sent, field, back, solved, resid, stacks, taps, kpad, blur_rows, blur_ops, gram_ops, step_ops,
     cheb, total, part, part_z, part_g, sum_z,
-    prior_sem, view_sem, send_sem, recv_sem, back_sem, ret_sem, z_send, z_recv, g_send, g_recv,
+    small_sem, prior_sem, view_sem, send_sem, recv_sem, back_sem, ret_sem, z_send, z_recv, g_send, g_recv,
 ):
     me = lax.axis_index("gz")
     row = lax.axis_index("gy")
@@ -160,8 +161,23 @@
             measured_ref.at[:, pl.ds(i * ROWS, ROWS), :], views.at[i], view_sem.at[i]
         )
 
+    small = [
+        pltpu.make_async_copy(source, target, small_sem.at[i])
+        for i, (source, target) in enumerate(
+            (
+                (mask_hbm, mask_ref),
+                (index_hbm, index_ref),
+                (index_hbm, index_row_ref),
+                (kernels_hbm, kernels_ref),
+            )
+        )
+    ]
+    for copy in small[:1]:
+        copy.start()
     for d in range(DEPTHS):
         prior_copy(d).start()
+    for copy in small[1:]:
+        copy.start()
 
     barrier = pltpu.get_barrier_semaphore()
     for offset in OFFSETS:
@@ -172,6 +188,8 @@
         )
 
     lane8 = lax.broadcasted_iota(jnp.int32, (ROWS, 128), 1)
+    for copy in small:
+        copy.wait()
     for d in range(DEPTHS):
         prior_copy(d).wait()
     for c in range(CHUNKS):
@@ -321,12 +339,14 @@
         sides = [field[c, pl.ds(pair * 2 + r, NZ, stride=ROWS), :] for r in range(2)]
         return jnp.concatenate(sides, axis=1)
 
-    def times(ops, value):
-        high, low = halves(value)
-        both = dot(ops[...], jnp.concatenate([high, low], axis=0))
+    def stacked(value):
+        return jnp.concatenate(halves(value), axis=0)
+
+    def times(ops, stack):
+        both = dot(ops[...], stack)
         return both[0:NZ] + both[NZ:]
 
-    total[...] = jnp.zeros((NZ, NZ), F32)
+    total[...] = jnp.zeros((2 * NZ, 2 * NZ), F32)
 
     @pl.loop(0, CHUNKS)
     def _(c):
@@ -335,14 +355,18 @@
         @pl.loop(0, ROWS // 2)
         def _(pair):
             at = c * (ROWS // 2) + pair
-            first = resid[at] - times(gram_ops, columns(c, pair))
-            resid[at] = first
-            total[...] += dot_nt(first, first)
+            first = resid[at] - times(gram_ops, stacked(columns(c, pair)))
+            stack = stacked(first)
+            stacks[at] = stack
+            total[...] += lax.dot_general(
+                stack, stack, (((1,), (1,)), ((), ())), preferred_element_type=F32
+            )
 
     lane1 = lax.broadcasted_iota(jnp.int32, (1, 128), 1)
     local = jnp.zeros((1, 128), F32)
+    square = total[0:NZ, 0:NZ] + (total[0:NZ, NZ:] + total[NZ:, 0:NZ]) + total[NZ:, NZ:]
     for k in range(2 * ITERS):
-        value = jnp.sum(cheb[k] * total[...], axis=0, keepdims=True)
+        value = jnp.sum(cheb[k] * square, axis=0, keepdims=True)
         local = jnp.where(lane1 == k, jnp.sum(value, axis=1, keepdims=True), local)
     part[0] = local
     part_z[row] = local
@@ -404,7 +428,7 @@
     def _(c):
         @pl.loop(0, ROWS // 2)
         def _(pair):
-            moved = columns(c, pair) + times(step_ops, resid[c * (ROWS // 2) + pair])
+            moved = columns(c, pair) + times(step_ops, stacks[c * (ROWS // 2) + pair])
             for r in range(2):
                 back[c, pl.ds(pair * 2 + r, NZ, stride=ROWS), :] = moved[:, r * 128 : (r + 1) * 128]
 
@@ -433,7 +457,16 @@
 
 
 def place_kernel(solved_ref, out_ref, sem):
-    copies = [pltpu.make_async_copy(solved_ref.at[d], out_ref.at[d], sem.at[d]) for d in range(DEPTHS)]
+    part = TILES * XT // 4
+    copies = [
+        pltpu.make_async_copy(
+            solved_ref.at[d, pl.ds(i * part, part)],
+            out_ref.at[d, pl.ds(i * part, part)],
+            sem.at[d * 4 + i],
+        )
+        for d in range(DEPTHS)
+        for i in range(4)
+    ]
     for copy in copies:
         copy.start()
     for copy in copies:
@@ -442,22 +475,26 @@
 
 def local(init, measured, mask, kernel_index, kernels):
     nx = TILES * XT
-    smem = pl.BlockSpec(memory_space=pltpu.SMEM)
     vmem = pl.BlockSpec(memory_space=pltpu.VMEM)
     hbm = pl.BlockSpec(memory_space=pltpu.HBM)
     dma = pltpu.SemaphoreType.DMA
     solved = pl.pallas_call(
         solve_kernel,
         out_shape=jax.ShapeDtypeStruct((DEPTHS, nx, 128), F32),
-        in_specs=[hbm, hbm, smem, smem, vmem, vmem],
+        in_specs=[hbm] * 5,
         out_specs=vmem,
         scratch_shapes=[
+            pltpu.SMEM((NY_BLOCKS, TILES), jnp.int32),
+            pltpu.SMEM((VIEWS * ZBANDS, TILES), jnp.int32),
+            pltpu.VMEM((VIEWS * ZBANDS, TILES), jnp.int32),
+            pltpu.VMEM((NK, TAPS), F32),
             pltpu.VMEM((2 * CHUNKS, VIEWS * NZ, ROWS, 128), F32),
             pltpu.VMEM((CHUNKS, PART, 128), F32),
             pltpu.VMEM((CHUNKS, PART, 128), F32),
             pltpu.VMEM((CHUNKS, PART, 128), F32),
             pltpu.VMEM((CHUNKS, PART, 128), F32),
             pltpu.VMEM((CHUNKS * ROWS // 2, NZ, 256), F32),
+            pltpu.VMEM((CHUNKS * ROWS // 2, 2 * NZ, 256), BF16),
             pltpu.VMEM((VIEWS * NZ, 128), F32),
             pltpu.VMEM((NK, 128), F32),
             pltpu.VMEM((VIEWS * NZ, NZ), F32),
@@ -465,11 +502,12 @@
             pltpu.VMEM((2 * NZ, 2 * NZ), BF16),
             pltpu.VMEM((2 * NZ, 2 * NZ), BF16),
             pltpu.VMEM((2 * ITERS, NZ, NZ), F32),
-            pltpu.VMEM((NZ, NZ), F32),
+            pltpu.VMEM((2 * NZ, 2 * NZ), F32),
             pltpu.VMEM((1, 1, 128), F32),
             pltpu.VMEM((4, 1, 128), F32),
             pltpu.VMEM((TILES, 1, 128), F32),
             pltpu.VMEM((1, 1, 128), F32),
+            dma((4,)),
             dma((DEPTHS,)),
             dma((2 * CHUNKS,)),
             dma((CHUNKS,)),
@@ -488,17 +526,18 @@
     )(
         init,
         measured.reshape(VIEWS * NZ, XT, YD),
-        mask.T,
-        kernel_index.reshape(VIEWS * ZBANDS, TILES),
-        kernel_index.reshape(VIEWS * ZBANDS, TILES),
-        kernels,
+        pltpu.with_memory_space_constraint(mask.T, pltpu.HBM),
+        pltpu.with_memory_space_constraint(
+            kernel_index.reshape(VIEWS * ZBANDS, TILES), pltpu.HBM
+        ),
+        pltpu.with_memory_space_constraint(kernels, pltpu.HBM),
     )
     return pl.pallas_call(
         place_kernel,
         out_shape=jax.ShapeDtypeStruct((DEPTHS, nx, 128), F32),
         in_specs=[vmem],
         out_specs=hbm,
-        scratch_shapes=[dma((DEPTHS,))],
+        scratch_shapes=[dma((4 * DEPTHS,))],
         compiler_params=pltpu.CompilerParams(vmem_limit_bytes=8 << 20),
         name="place",
     )(solved)

time: 79.2 us -> 76 us (0.960)
  local copies, waits for them, and re-layouts: 2.1 us -> 0 us
  Pallas kernels: 76.5 us -> 75.6 us
    unnamed x6 -> x0, local copies, waits for them, and re-layouts: 2.1 us -> none
    pallas_call x1, Pallas kernels: 74.5 us -> 73.4 us  [local(): pl.pallas_call(solve_kernel, out_shape=jax.ShapeDtypeStruct((DEPTHS, nx,...]
where the time goes in v2:
time: 76 us; the launch traced here: 75.6 us
  Pallas kernels  75.6 us (99%)
    pallas_call x1, Pallas kernels, local(): pl.pallas_call(solve_kernel, out_shape=jax.ShapeDtypeStruct((DEPTHS, nx,...  73.4 us
    pallas_call x1, Pallas kernels, local(): pl.pallas_call(place_kernel, out_shape=jax.ShapeDtypeStruct((DEPTHS, nx,...  2.14 us

profile of v2, /device:TPU:1, one launch (start us, length us, event | category | flops | bytes accessed | tf_op | source)
XLA Modules:
  0.0 75.6 jit_solution(3105600044061266969)
XLA Ops:
  0.0 73.4 %solve.1.solved_ref = f32[4,2048,128]{2,1,0:T(8,128)S(1)} custom-call(f32[4,2048,128]{2,1,0:T(8,128)} %init_ref.1, f32[512,64,128]{2,1,0:T(8,128)} %bitcast.3, s32[8,32]{1,0:T(8,128)} %bitcast.5, s32[32,32]{1,0:T(8,128)} %bitcast.4, f32[16,31]{1,0:T(8,128)} %kernels_hbm.1), custom_call_target="tpu_custom_call" | custom-call | tf_op jit(solution)/shard_map/solve/pallas_call | solution.py:481
  73.4 2.1 %place.1 = f32[4,2048,128]{2,1,0:T(8,128)} custom-call(f32[4,2048,128]{2,1,0:T(8,128)S(1)} %solve.1.solved_ref), custom_call_target="tpu_custom_call" | custom-call | tf_op jit(solution)/shard_map/place/pallas_call | solution.py:535

commit v3 on v2

--- a/solution.py
+++ b/solution.py
@@ -55,6 +55,14 @@
 def halves(value):
     high = value.astype(BF16)
     return high, (value - high.astype(F32)).astype(BF16)
+
+
+def put_ops(ops, matrix):
+    high, low = halves(matrix)
+    ops[0:NZ, 0:NZ] = high
+    ops[0:NZ, NZ:] = high
+    ops[NZ:, 0:NZ] = low
+    ops[NZ:, NZ:] = jnp.zeros((NZ, NZ), BF16)
 
 
 def pack(low_rows, high_rows, upper, lane):
@@ -137,7 +145,7 @@
 
 def solve_kernel(
     init_ref, measured_ref, mask_hbm, index_hbm, kernels_hbm, prior,
-    mask_ref, index_ref, index_row_ref, kernels_ref, views, sent, field, back, solved, resid, stacks, taps, kpad, blur_rows, blur_ops, gram_ops, step_ops,
+    mask_ref, index_ref, index_row_ref, kernels_ref, views, sent, field, back, solved, resid, stacks, taps, kpad, blur_rows, blur_ops, gram_ops, step_ops, cheb_ops, early,
     cheb, total, part, part_z, part_g, sum_z,
     small_sem, prior_sem, view_sem, send_sem, recv_sem, back_sem, ret_sem, z_send, z_recv, g_send, g_recv,
 ):
@@ -271,11 +279,7 @@
     for v in range(1, VIEWS):
         at = pl.ds(v * NZ, NZ)
         grams = grams + dot(taps[at, :], blur_rows[at, :], HIGHEST)
-    high, low = halves(grams)
-    gram_ops[0:NZ, 0:NZ] = high
-    gram_ops[0:NZ, NZ:] = high
-    gram_ops[NZ:, 0:NZ] = low
-    gram_ops[NZ:, NZ:] = jnp.zeros((NZ, NZ), BF16)
+    put_ops(gram_ops, grams)
 
     bins = lax.broadcasted_iota(jnp.int32, (NK, TILES), 0)
     span = lax.broadcasted_iota(jnp.int32, (3 * ZBW, 128), 0)
@@ -310,6 +314,8 @@
     cheb[5] = 2.0 * dot(cheb[2], cheb[3], HIGHEST) - cheb[1]
     cheb[6] = 2.0 * dot(cheb[3], cheb[3], HIGHEST) - eye
     cheb[7] = 2.0 * dot(cheb[3], cheb[4], HIGHEST) - cheb[1]
+    for j in range(1, ITERS):
+        put_ops(cheb_ops.at[j - 1], cheb[j])
 
     mine = jnp.full((NZ, 128), mask_ref[2 * row + 1, me], jnp.int32) != 0
 
@@ -358,6 +364,7 @@
             first = resid[at] - times(gram_ops, stacked(columns(c, pair)))
             stack = stacked(first)
             stacks[at] = stack
+            resid[at] = first
             total[...] += lax.dot_general(
                 stack, stack, (((1,), (1,)), ((), ())), preferred_element_type=F32
             )
@@ -382,6 +389,12 @@
         )
         copy.start()
         hops.append(copy)
+
+    @pl.loop(0, ROWS // 2)
+    def _(pair):
+        for j in range(ITERS - 1):
+            early[j, pair] = times(cheb_ops.at[j], stacks[pair])
+
     for copy in hops:
         copy.wait()
     along = (part_z[0] + part_z[1]) + (part_z[2] + part_z[3])
@@ -415,25 +428,37 @@
     ]
     weights = cg_weights(moments, centre, half)
 
+    def put_back(c, pair, step):
+        moved = columns(c, pair) + step
+        for r in range(2):
+            back[c, pl.ds(pair * 2 + r, NZ, stride=ROWS), :] = moved[:, r * 128 : (r + 1) * 128]
+
+    def send_back(c):
+        solved[c, own, :] = back[c, own, :]
+        send_chunk(back, solved, c, back_sem, ret_sem)
+
+    wide = [jnp.concatenate([weight, weight], axis=1) for weight in weights]
+
+    @pl.loop(0, ROWS // 2)
+    def _(pair):
+        step = wide[0] * resid[pair]
+        for j in range(1, ITERS):
+            step = step + wide[j] * early[j - 1, pair]
+        put_back(0, pair, step)
+
+    send_back(0)
     poly = weights[0] * cheb[0]
     for j in range(1, ITERS):
         poly = poly + weights[j] * cheb[j]
-    high, low = halves(poly)
-    step_ops[0:NZ, 0:NZ] = high
-    step_ops[0:NZ, NZ:] = high
-    step_ops[NZ:, 0:NZ] = low
-    step_ops[NZ:, NZ:] = jnp.zeros((NZ, NZ), BF16)
-
-    @pl.loop(0, CHUNKS)
+    put_ops(step_ops, poly)
+
+    @pl.loop(1, CHUNKS)
     def _(c):
         @pl.loop(0, ROWS // 2)
         def _(pair):
-            moved = columns(c, pair) + times(step_ops, stacks[c * (ROWS // 2) + pair])
-            for r in range(2):
-                back[c, pl.ds(pair * 2 + r, NZ, stride=ROWS), :] = moved[:, r * 128 : (r + 1) * 128]
-
-        solved[c, own, :] = back[c, own, :]
-        send_chunk(back, solved, c, back_sem, ret_sem)
+            put_back(c, pair, times(step_ops, stacks[c * (ROWS // 2) + pair]))
+
+        send_back(c)
 
     @pl.loop(0, CHUNKS)
     def _(c):
@@ -501,6 +526,8 @@
             pltpu.VMEM((2 * NZ, VIEWS * NZ), BF16),
             pltpu.VMEM((2 * NZ, 2 * NZ), BF16),
             pltpu.VMEM((2 * NZ, 2 * NZ), BF16),
+            pltpu.VMEM((ITERS - 1, 2 * NZ, 2 * NZ), BF16),
+            pltpu.VMEM((ITERS - 1, ROWS // 2, NZ, 256), F32),
             pltpu.VMEM((2 * ITERS, NZ, NZ), F32),
             pltpu.VMEM((2 * NZ, 2 * NZ), F32),
             pltpu.VMEM((1, 1, 128), F32),

time: 76 us -> 75.5 us (level)
  no operation moved by 1% of the time
where the time goes in v3:
time: 75.5 us; the launch traced here: 75.1 us
  Pallas kernels  75.1 us (99%)
    pallas_call x1, Pallas kernels, local(): pl.pallas_call(solve_kernel, out_shape=jax.ShapeDtypeStruct((DEPTHS, nx,...  72.9 us
    pallas_call x1, Pallas kernels, local(): pl.pallas_call(place_kernel, out_shape=jax.ShapeDtypeStruct((DEPTHS, nx,...  2.14 us

profile of v3, /device:TPU:1, one launch (start us, length us, event | category | flops | bytes accessed | tf_op | source)
XLA Modules:
  0.0 75.1 jit_solution(3629814195041313088)
XLA Ops:
  0.0 72.9 %solve.1.solved_ref = f32[4,2048,128]{2,1,0:T(8,128)S(1)} custom-call(f32[4,2048,128]{2,1,0:T(8,128)} %init_ref.1, f32[512,64,128]{2,1,0:T(8,128)} %bitcast.3, s32[8,32]{1,0:T(8,128)} %bitcast.5, s32[32,32]{1,0:T(8,128)} %bitcast.4, f32[16,31]{1,0:T(8,128)} %kernels_hbm.1), custom_call_target="tpu_custom_call" | custom-call | tf_op jit(solution)/shard_map/solve/pallas_call | solution.py:506
  72.9 2.1 %place.1 = f32[4,2048,128]{2,1,0:T(8,128)} custom-call(f32[4,2048,128]{2,1,0:T(8,128)S(1)} %solve.1.solved_ref), custom_call_target="tpu_custom_call" | custom-call | tf_op jit(solution)/shard_map/place/pallas_call | solution.py:562

commit v4 on v3

--- a/solution.py
+++ b/solution.py
@@ -157,6 +157,8 @@
 
     def peer(offset):
         dx, dy, dc = offset
+        sign = 1 - 2 * my_core
+        dx, dy = dx * sign + RINGX, dy * sign + RINGY
         return (
             lax.rem(my_y + dy, RINGY) * RINGX + lax.rem(my_x + dx, RINGX)
         ) * CORES + lax.rem(my_core + dc, CORES)

time: 75.5 us -> 75.2 us (level)
  no operation moved by 1% of the time
where the time goes in v4:
time: 75.2 us; the launch traced here: 75 us
  Pallas kernels  75 us (100%)
    pallas_call x1, Pallas kernels, local(): pl.pallas_call(solve_kernel, out_shape=jax.ShapeDtypeStruct((DEPTHS, nx,...  72.9 us
    pallas_call x1, Pallas kernels, local(): pl.pallas_call(place_kernel, out_shape=jax.ShapeDtypeStruct((DEPTHS, nx,...  2.14 us

profile of v4, /device:TPU:1, one launch (start us, length us, event | category | flops | bytes accessed | tf_op | source)
XLA Modules:
  0.0 75.0 jit_solution(2938852588489963470)
XLA Ops:
  0.0 72.9 %solve.1.solved_ref = f32[4,2048,128]{2,1,0:T(8,128)S(1)} custom-call(f32[4,2048,128]{2,1,0:T(8,128)} %init_ref.1, f32[512,64,128]{2,1,0:T(8,128)} %bitcast.3, s32[8,32]{1,0:T(8,128)} %bitcast.5, s32[32,32]{1,0:T(8,128)} %bitcast.4, f32[16,31]{1,0:T(8,128)} %kernels_hbm.1), custom_call_target="tpu_custom_call" | custom-call | tf_op jit(solution)/shard_map/solve/pallas_call | solution.py:508
  72.9 2.1 %place.1 = f32[4,2048,128]{2,1,0:T(8,128)} custom-call(f32[4,2048,128]{2,1,0:T(8,128)S(1)} %solve.1.solved_ref), custom_call_target="tpu_custom_call" | custom-call | tf_op jit(solution)/shard_map/place/pallas_call | solution.py:564
